TPU v7x, 32 devices: a whole 2x2x4 slice. The times are simulated.
32 devices in a mesh: seq: 16 (over z, x, core), head: 2 (over y).
Axes of the slice: x: 2, y: 2, z: 4, core: 2. Of those that a mesh axis runs over, the one named last changes fastest.
Arguments:
- qkv: bfloat16 [3, 8192, 4096], P(None, ('seq', 'head')), may hold values from -6 to 6
- send_rows: int32 [16, 16, 40], P('seq'), may hold values from -1 to 511, as said below
- recv_pos: int32 [16, 16, 40], P('seq'), may hold values from -1 to 511, as said below
- req_lengths: int32 [4], replicated, may hold values from 1 to 4096, 8192 in all
- norm_gain: float32 [4096], P('head'), may hold values from 0.5 to 1.5
Outputs:
- attn_out: bfloat16 [8192, 4096], P('seq', 'head')
Inputs may be any that keep to these rules, and one draw needn't show every extreme that they name: send_rows[l, o, c] is a row of loader group l (rows l * 512 to l * 512 + 511 of qkv, counted from the group's first) sent to owner o in slot c, or -1 for an empty slot; used slots come first. Every row of a group is sent exactly once. At most 40 rows go from one group to one owner, and in every draw some pairs carry exactly 40, so that every group sends and every owner receives 40 rows from one pair. The number of rows from group l to owner o depends only on (o - l) modulo the number of groups. recv_pos[o, l, c] is the position within owner o's block of 512 packed positions where slot c from group l lands, and -1 exactly where send_rows[l, o, c] is -1; every position of a block is filled exactly once.
All inputs are finite; a program needn't handle non-finite values.
Results may differ from a plain program's by a relative error of at most 0.003.
Values may be sent and summed in bfloat16 or wider, within the bound.
No kernel may reach another device: no remote copies, remote signals or barrier semaphores. Data moves between devices by JAX's collectives and lax.ppermute only.
A program may use at most 128 MiB of HBM per device.

v0:
```python
import jax
import jax.numpy as jnp
from jax import lax
from jax.sharding import PartitionSpec as P

HEAD_DIM = 128
norm_eps = 1e-06


def prefix(shard, axis, combine, identity):
    length, position = (lax.axis_size(axis), lax.axis_index(axis))
    everything = jax.tree.map(lambda part: lax.all_gather(part, axis), shard)
    start = jax.tree.map(
        lambda part, zero: jnp.broadcast_to(jnp.asarray(zero, part.dtype), part.shape),
        shard,
        identity,
    )

    def lap(k, before):
        reached = k < position
        new = combine(before, jax.tree.map(lambda part: part[k], everything))
        return jax.tree.map(lambda a, b: jnp.where(reached, a, b), new, before)

    return lax.fori_loop(0, length, lap, start)


def place_rows(incoming, land_rows, tok_rows):
    row_width = incoming.shape[-1]
    planes = incoming.shape[0]
    flat_rows = incoming.reshape(planes, -1, row_width)
    land_index = jnp.where(land_rows < 0, tok_rows, land_rows).reshape(-1)
    blank_rows = jnp.zeros((planes, tok_rows, row_width), incoming.dtype)
    return blank_rows.at[:, land_index].set(flat_rows, mode="drop")


def carry_combine(earlier, later):
    return (later[0] + (1.0 - later[1]) * earlier[0], jnp.maximum(earlier[1], later[1]))


def on_device(qkv, send_rows, recv_pos, req_lengths, norm_gain):
    seq_count = lax.axis_size("seq")
    slot_count = send_rows.shape[2]
    pick_rows = jnp.maximum(send_rows[0], 0).reshape(-1)
    land_rows = recv_pos[0]
    grouped = lax.all_to_all(qkv, "head", split_axis=2, concat_axis=1, tiled=True)
    outgoing = jnp.take(grouped, pick_rows, axis=1).reshape(
        3, seq_count, slot_count, grouped.shape[2]
    )
    arrived = lax.all_to_all(outgoing, "seq", split_axis=1, concat_axis=1, tiled=True)
    packed = place_rows(arrived, land_rows, grouped.shape[1])
    query, keys, values = (packed[0], packed[1], packed[2])
    tok_rows = keys.shape[0]
    head_count = keys.shape[1] // HEAD_DIM
    first_row = lax.axis_index("seq") * tok_rows
    req_ends = jnp.cumsum(req_lengths)
    req_starts = req_ends - req_lengths
    positions = first_row + jnp.arange(tok_rows, dtype=jnp.int32)
    segment = jnp.sum((req_starts[None, :] <= positions[:, None]).astype(jnp.int32), axis=1) - 1
    prev_segment = jnp.sum((req_starts < first_row).astype(jnp.int32)) - 1
    inside = jnp.any((req_starts >= first_row) & (req_starts < first_row + tok_rows))
    has_start = jnp.where(inside, 1.0, 0.0).astype(jnp.float32)
    carried_mask = segment == prev_segment
    tail_mask = segment == segment[tok_rows - 1]
    causal = (positions[None, :] <= positions[:, None]) & (segment[None, :] == segment[:, None])
    tail_keys = jnp.where(tail_mask[:, None], keys, jnp.zeros_like(keys))
    update = jnp.einsum(
        "shd,she->hde",
        tail_keys.reshape(tok_rows, head_count, HEAD_DIM),
        values.reshape(tok_rows, head_count, HEAD_DIM),
        preferred_element_type=jnp.float32,
    )
    identity = (jnp.zeros_like(update), jnp.zeros((), jnp.float32))
    carried_pair = prefix((update, has_start), "seq", carry_combine, identity)
    carried = carried_pair[0]
    outputs = []
    for number in range(head_count):
        columns = slice(number * HEAD_DIM, (number + 1) * HEAD_DIM)
        query_head = query[:, columns]
        key_head = keys[:, columns]
        value_head = values[:, columns]
        scores = lax.dot_general(
            query_head, key_head, (((1,), (1,)), ((), ())), preferred_element_type=jnp.float32
        )
        weights = jnp.where(causal, scores, 0.0).astype(jnp.bfloat16)
        local_term = jnp.dot(weights, value_head, preferred_element_type=jnp.float32)
        carried_term = jnp.dot(
            query_head.astype(jnp.float32),
            carried[number],
            precision=lax.Precision.HIGHEST,
            preferred_element_type=jnp.float32,
        )
        raw_out = local_term + jnp.where(carried_mask[:, None], carried_term, 0.0)
        inv_rms = lax.rsqrt(jnp.mean(raw_out * raw_out, axis=1, keepdims=True) + norm_eps)
        outputs.append((raw_out * inv_rms * norm_gain[columns][None, :]).astype(jnp.bfloat16))
    return jnp.concatenate(outputs, axis=1)


def solution(mesh):
    return jax.shard_map(
        on_device,
        mesh=mesh,
        in_specs=(
            P(None, ("seq", "head"), None),
            P("seq", None, None),
            P("seq", None, None),
            P(),
            P("head"),
        ),
        out_specs=P("seq", "head"),
        check_vma=False,
    )
```

profile of v0, /device:TPU:0, one launch (start us, length us, event | category | flops | bytes accessed | tf_op | source)
XLA Modules:
  0.0 782.3 jit_solution(8094631923778563405)
XLA Ops:
  6.5 13.1 %copy.40 = bf16[3,256,4096]{1,0,2:T(4,128)(2,1)} copy(bf16[3,256,4096]{2,1,0:T(8,128)(2,1)} %param.7) | data formatting | bytes 12582912 | tf_op args[0]
  19.6 7.1 all-to-all-start
  26.8 93.7 %all-to-all-done = bf16[3,256,4096]{1,0,2:T(4,128)(2,1)} async-done(((bf16[3,256,4096]{1,0,2:T(4,128)(2,1)}), bf16[3,256,4096]{1,0,2:T(4,128)(2,1)}, u32[]{:S(2)}, u32[]{:S(2)}) %all-to-all-start) | async-done | bytes 6291488 | tf_op jit(solution)/shard_map/all_to_all | solution.py:45
  120.6 7.0 copy.41
  127.5 8.7 %copy.42 = bf16[3,2,256,2048]{3,2,1,0:T(8,128)(2,1)} copy(bf16[3,2,256,2048]{2,3,1,0:T(8,128)(2,1)} %bitcast.90) | data formatting | bytes 12582912 | tf_op jit(solution)/shard_map/all_to_all | solution.py:45
  136.2 11.5 %copy.43 = bf16[3,512,2048]{2,0,1:T(4,128)(2,1)} copy(bf16[3,512,2048]{2,1,0:T(8,128)(2,1)} %bitcast.91) | data formatting | bytes 12582912 | tf_op jit(solution)/shard_map/all_to_all | solution.py:45
  147.7 24.7 %gather_fusion = bf16[640,3,2048]{2,1,0:T(4,128)(2,1)} fusion(bf16[3,512,2048]{2,0,1:T(4,128)(2,1)} %copy.43, s32[1024]{0:T(1024)S(1)} %pad_clamp_fusion), kind=kCustom, calls=%fused_computation | custom fusion | bytes 15731200 | tf_op jit(solution)/shard_map/jit(_take)/gather | solution.py:46
  172.5 16.3 %copy_select_fusion = bf16[3,16,40,2048]{3,2,0,1:T(8,128)(2,1)} fusion(bf16[3,16,40,2048]{3,0,2,1:T(4,128)(2,1)} %bitcast.88, pred[16,40]{1,0:T(8,128)(4,1)S(1)} %compare_bitcast_fusion), kind=kLoop, calls=%fused_computation.4 | loop fusion | flops 3932160 | bytes 15729280 | tf_op jit(solution)/shard_map/jit(_take)/select_n | solution.py:46
  188.7 6.2 all-to-all-start.1
  198.7 137.9 %all-to-all-done.1 = bf16[3,16,40,2048]{3,2,0,1:T(8,128)(2,1)} async-done(((bf16[3,16,40,2048]{3,2,0,1:T(8,128)(2,1)}), bf16[3,16,40,2048]{3,2,0,1:T(8,128)(2,1)}, u32[]{:S(2)}, u32[]{:S(2)}) %all-to-all-start.1) | async-done | bytes 7864352 | tf_op jit(solution)/shard_map/all_to_all | solution.py:49
  336.6 4.2 copy.45
  340.8 25.5 %copy.46 = bf16[640,3,2048]{2,1,0:T(4,128)(2,1)} copy(bf16[640,3,2048]{2,0,1:T(8,128)(2,1)S(1)} %bitcast.89) | data formatting | bytes 15728640 | tf_op jit(solution)/shard_map/reshape | solution.py:30
  366.3 7.6 broadcast_in_dim.178
  373.9 85.0 %scatter_fusion = bf16[3,512,2048]{2,0,1:T(4,128)(2,1)} fusion(bf16[3,512,2048]{2,0,1:T(4,128)(2,1)} %broadcast_in_dim.178, s32[640]{0:T(1024)S(1)} %fusion.213, bf16[640,3,2048]{2,1,0:T(4,128)(2,1)} %copy.46), kind=kCustom, calls=%fused_computation.1 | custom fusion | bytes 23595520 | tf_op jit(solution)/shard_map/scatter | solution.py:33
  459.0 20.8 %fusion.232 = (bf16[1,512,2048]{2,0,1:T(2,128)(2,1)}, bf16[1,512,2048]{2,0,1:T(2,128)(2,1)}, bf16[1,512,2048]{2,0,1:T(2,128)(2,1)}) fusion(bf16[3,512,2048]{2,0,1:T(4,128)(2,1)} %scatter_fusion), kind=kLoop, calls=%fused_computation.301 | loop fusion | bytes 12582912 | tf_op jit(solution)/shard_map/slice | solution.py:51
  479.8 9.0 %copy.47 = bf16[1,512,2048]{1,2,0:T(8,128)(2,1)S(1)} copy(bf16[1,512,2048]{2,0,1:T(2,128)(2,1)} %get-tuple-element.130) | data formatting | bytes 4194304 | tf_op jit(solution)/shard_map/slice | solution.py:51
  488.8 10.5 %copy.48 = bf16[1,512,2048]{1,2,0:T(8,128)(2,1)} copy(bf16[1,512,2048]{2,0,1:T(2,128)(2,1)} %get-tuple-element.131) | data formatting | bytes 4194304 | tf_op jit(solution)/shard_map/slice | solution.py:51
  499.3 3.3 fusion.1
  504.5 63.3 %all-reduce = f32[16]{0:T(128)S(1)} all-reduce(f32[16]{0:T(128)S(1)} %dynamic-update-slice), channel_id=1, replica_groups=mesh['seq'=16,'head'=2] {'seq'}, use_global_device_ids=true, to_apply=%add | all-reduce | flops 16 | bytes 128
  567.8 3.6 copy.59
  571.5 6.9 copy_bitcast_fusion
  578.4 80.6 %all-gather.3.cloned.1.call-done = f32[256,128,128]{2,1,0:T(8,128)} async-done(((f32[16,128,128]{2,1,0:T(8,128)}), f32[256,128,128]{2,1,0:T(8,128)}) %all-gather.3.cloned.1.call-update) | async-done | bytes 16777232 | tf_op jit(solution)/shard_map/all_gather | solution.py:12
  658.9 54.5 %while.14 = (s32[]{:T(128)}, f32[16,128,128]{2,1,0:T(8,128)S(1)}, s32[]{:T(128)}, f32[16,16,128,128]{3,2,1,0:T(8,128)}, f32[16]{0:T(128)S(1)}, /*index=5*/s32[]{:T(128)}, f32[1]{0:T(128)}, s32[]{:T(128)}) while((s32[]{:T(128)}, f32[16,128,128]{2,1,0:T(8,128)S(1)}, s32[]{:T(128)}, f32[16,16,128,128]{3,2,1,0:T(8,128)}, ...), condition=%wide.region_6.7_spmd.clone, body=%wide.region_5.6_spmd.clone.sunk | while | flops 1048581 | bytes 3145873 | solution.py:24
  660.2 2.1 fusion.300
  663.6 2.1 fusion.300
  667.0 2.1 fusion.300
  670.4 2.1 fusion.300
  673.8 2.1 fusion.300
  677.2 2.1 fusion.300
  680.6 2.1 fusion.300
  684.0 2.1 fusion.300
  687.4 2.1 fusion.300
  690.8 2.1 fusion.300
  694.1 2.1 fusion.300
  697.5 2.1 fusion.300
  700.9 2.1 fusion.300
  704.3 2.1 fusion.300
  707.7 2.1 fusion.300
  711.1 2.1 fusion.300
  718.6 1.0 convolution_select_fusion.24
  721.7 1.0 convolution_select_fusion.27
  724.8 1.0 convolution_select_fusion.30
  728.9 1.0 convolution_select_fusion.18
  729.9 1.7 multiply_reduce_fusion.3
  731.6 2.4 multiply_reduce_fusion.4
  734.1 2.3 multiply_reduce_fusion.5
  736.3 2.3 multiply_reduce_fusion.6
  738.6 2.3 multiply_reduce_fusion.7
  740.9 2.3 multiply_reduce_fusion.8
  743.2 2.3 multiply_reduce_fusion.9
  745.5 2.3 multiply_reduce_fusion.10
  747.8 2.3 multiply_reduce_fusion.11
  750.1 2.3 multiply_reduce_fusion.12
  752.4 2.3 multiply_reduce_fusion.13
  754.7 2.3 multiply_reduce_fusion.14
  757.0 2.3 multiply_reduce_fusion.15
  759.3 2.3 multiply_reduce_fusion
  761.6 2.2 multiply_reduce_fusion.2
  763.8 2.2 multiply_reduce_fusion.1
  766.1 1.1 fusion.69
  767.3 1.1 fusion.70
  769.4 1.1 fusion.72
  770.5 1.1 fusion.73
  772.7 2.4 copy.50
  (137 shorter events, 28.7 us)
Async XLA Ops:
  19.6 7.1 copy-start.25
  19.6 100.9 %all-to-all-start = ((bf16[3,256,4096]{1,0,2:T(4,128)(2,1)}), bf16[3,256,4096]{1,0,2:T(4,128)(2,1)}, u32[]{:S(2)}, u32[]{:S(2)}) async-start(bf16[3,256,4096]{1,0,2:T(4,128)(2,1)} %copy.40), calls=%async_computation | async-start | bytes 16777216 | tf_op jit(solution)/shard_map/all_to_all | solution.py:45
  188.7 6.3 copy-start.28
  188.7 7.8 %copy-start.26 = (s32[1,16,40]{2,1,0:T(8,128)S(1)}, s32[1,16,40]{2,1,0:T(8,128)}, u32[]{:S(2)}) copy-start(s32[1,16,40]{2,1,0:T(8,128)} %param.9) | copy-start | bytes 7684
  188.7 147.8 %all-to-all-start.1 = ((bf16[3,16,40,2048]{3,2,0,1:T(8,128)(2,1)}), bf16[3,16,40,2048]{3,2,0,1:T(8,128)(2,1)}, u32[]{:S(2)}, u32[]{:S(2)}) async-start(bf16[3,16,40,2048]{3,2,0,1:T(8,128)(2,1)} %copy_select_fusion), calls=%async_computation.1 | async-start | bytes 15728640 | tf_op jit(solution)/shard_map/all_to_all | solution.py:49
  195.0 464.0 %all-gather.3.cloned.1.call-start = ((), (), s32[]{:S(2)}) async-start(), calls=%async_computation.2 | async-start | bytes 17825792 | tf_op jit(solution)/shard_map/all_gather | solution.py:12
  499.3 3.3 copy-start.29
  499.3 68.5 %copy-start.27 = (f32[2048]{0:T(1024)S(1)}, f32[2048]{0:T(1024)}, u32[]{:S(2)}) copy-start(f32[2048]{0:T(1024)} %param.11) | copy-start | bytes 24580
  567.8 3.7 copy-start
  729.9 4.1 copy-start.24
  731.6 4.7 copy-start.23
  734.0 4.6 copy-start.22
  736.3 4.6 copy-start.21
  738.6 4.6 copy-start.20
  740.9 4.6 copy-start.19
  743.2 4.6 copy-start.18
  745.5 4.6 copy-start.17
  747.8 4.6 copy-start.16
  750.1 4.6 copy-start.15
  752.4 4.6 copy-start.14
  754.7 4.6 copy-start.13
  757.0 4.6 copy-start.12
  759.3 4.5 copy-start.11
  766.0 5.5 copy-start.10
  766.1 5.6 copy-start.7
  766.1 5.7 copy-start.6
  766.1 5.8 copy-start.4
  766.1 5.9 copy-start.3
  766.1 6.0 copy-start.2
  767.3 5.0 copy-start.1
  769.4 3.0 copy-start.9
  770.5 2.0 copy-start.8
  771.6 1.0 copy-start.5
Sparse Core Ops, SparseCore 0:
  502.7 156.1 all-gather.2
where the time goes:
time: 794 us; the launch traced here: 782 us
  waiting for transfers between devices  312 us (39%)
  local copies, waits for them, and re-layouts  253 us (32%)
  blocking collectives  63.3 us (8%)
  other arithmetic  59.2 us (7%)
  matrix products  55.6 us (7%)
  between operations  15.6 us (2%)
  starting transfers between devices  13.3 us (2%)
  loops' own time  10.4 us (1%)
    all_to_all x1, waiting for transfers between devices, on_device(): lax.all_to_all(outgoing, 'seq', split_axis=1, concat_axis=1, tiled=True)  138 us
    all_to_all x1, waiting for transfers between devices, on_device(): lax.all_to_all(qkv, 'head', split_axis=2, concat_axis=1, tiled=True)  93.7 us
    scatter x1, local copies, waits for them, and re-layouts, place_rows(): return blank_rows.at[:, land_index].set(flat_rows, mode='drop')  85 us
    all_gather x1, waiting for transfers between devices, prefix(): everything = jax.tree.map(lambda part: lax.all_gather(part, axis), shard)  80.6 us
    unnamed x1, blocking collectives  63.3 us
    slice x3, local copies, waits for them, and re-layouts, on_device(): query, keys, values = (packed[0], packed[1], packed[2])  40.3 us
    dot_general x16, matrix products, on_device(): jnp.dot(weights, value_head, preferred_element_type=jnp.float32)  35.8 us
    select_n x16, other arithmetic, lap(): return jax.tree.map(lambda a, b: jnp.where(reached, a, b), new, before)  34.2 us
  transfers between devices with their start and end apart: 3, of which 3 were waited for; matrix products, arithmetic and copies ran while one was open for 2% of the time, Pallas kernels for 0%

commit v1 on v0

--- a/solution.py
+++ b/solution.py
@@ -5,6 +5,17 @@
 
 HEAD_DIM = 128
 norm_eps = 1e-06
+
+
+def split_up(x, dim, count):
+    before, after = (x.shape[:dim], x.shape[dim + 1 :])
+    return jnp.moveaxis(x.reshape(*before, count, -1, *after), dim, 0)
+
+
+def laid_out(parts, dim):
+    lengths = list(parts.shape[1:])
+    lengths[dim] *= parts.shape[0]
+    return jnp.moveaxis(parts, 0, dim).reshape(lengths)
 
 
 def prefix(shard, axis, combine, identity):
@@ -46,7 +57,14 @@
     outgoing = jnp.take(grouped, pick_rows, axis=1).reshape(
         3, seq_count, slot_count, grouped.shape[2]
     )
-    arrived = lax.all_to_all(outgoing, "seq", split_axis=1, concat_axis=1, tiled=True)
+    size, index = (lax.axis_size("seq"), lax.axis_index("seq"))
+    blocks = split_up(outgoing, 1, size)
+    outs = [blocks[index]]
+    for step in range(1, size):
+        sent = blocks[index ^ step]
+        outs.append(lax.ppermute(sent, "seq", [(i, i ^ step) for i in range(size)]))
+    blocks = jnp.stack(outs)[index ^ jnp.arange(size)]
+    arrived = laid_out(blocks, 1)
     packed = place_rows(arrived, land_rows, grouped.shape[1])
     query, keys, values = (packed[0], packed[1], packed[2])
     tok_rows = keys.shape[0]

time: 794 us -> 833 us (1.049)
  starting transfers between devices: 13.3 us -> 70.3 us
  waiting for transfers between devices: 312 us -> 256 us
  local copies, waits for them, and re-layouts: 253 us -> 296 us
  other arithmetic: 59.2 us -> 50.6 us
    all_to_all x1 -> x0, waiting for transfers between devices: 138 us -> none  [on_device(): lax.all_to_all(outgoing, 'seq', split_axis=1, concat_axis=1, tiled=True)]
    ppermute x0 -> x15, waiting for transfers between devices: none -> 78.7 us  [on_device(): outs.append(lax.ppermute(sent, 'seq', [(i, i ^ step) for i in range(size)]))]
    ppermute x0 -> x15, starting transfers between devices: none -> 63.1 us  [on_device(): outs.append(lax.ppermute(sent, 'seq', [(i, i ^ step) for i in range(size)]))]
    another operation x0 -> x18, local copies, waits for them, and re-layouts: none -> 38.1 us  [the longest x1 25.3 us: place_rows(): flat_rows = incoming.reshape(planes, -1, row_width)]
    reshape x1 -> x0, local copies, waits for them, and re-layouts: 25.5 us -> none  [place_rows(): flat_rows = incoming.reshape(planes, -1, row_width)]
    gather x0 -> x1, local copies, waits for them, and re-layouts: none -> 17.6 us  [on_device(): blocks = jnp.stack(outs)[index ^ jnp.arange(size)]]
    unnamed x66 -> x81, local copies, waits for them, and re-layouts: 25 us -> 38 us
    select_n x1, other arithmetic: 16.3 us -> 7.52 us  [on_device(): jnp.take(grouped, pick_rows, axis=1)]
  transfers between devices with their start and end apart: 3 -> 17, of which waited for: 3 -> 8; matrix products, arithmetic and copies ran while one was open for 2% -> 4% of each run, Pallas kernels for 0% -> 0%
where the time goes in v1:
time: 833 us; the launch traced here: 820 us
  local copies, waits for them, and re-layouts  296 us (36%)
  waiting for transfers between devices  256 us (31%)
  starting transfers between devices  70.3 us (8%)
  blocking collectives  64.2 us (8%)
  matrix products  55.3 us (7%)
  other arithmetic  50.6 us (6%)
  between operations  16 us (2%)
  loops' own time  11.7 us (1%)
    all_to_all x1, waiting for transfers between devices, on_device(): lax.all_to_all(qkv, 'head', split_axis=2, concat_axis=1, tiled=True)  89.8 us
    all_gather x1, waiting for transfers between devices, prefix(): everything = jax.tree.map(lambda part: lax.all_gather(part, axis), shard)  87.7 us
    scatter x1, local copies, waits for them, and re-layouts, place_rows(): return blank_rows.at[:, land_index].set(flat_rows, mode='drop')  85.1 us
    ppermute x15, waiting for transfers between devices, on_device(): outs.append(lax.ppermute(sent, 'seq', [(i, i ^ step) for i in range(size)]))  78.7 us
    unnamed x1, blocking collectives  64.2 us
    ppermute x15, starting transfers between devices, on_device(): outs.append(lax.ppermute(sent, 'seq', [(i, i ^ step) for i in range(size)]))  63.1 us
    slice x3, local copies, waits for them, and re-layouts, on_device(): query, keys, values = (packed[0], packed[1], packed[2])  40.2 us
    unnamed x81, local copies, waits for them, and re-layouts  38 us
  transfers between devices with their start and end apart: 17, of which 8 were waited for; matrix products, arithmetic and copies ran while one was open for 4% of the time, Pallas kernels for 0%

profile of v1, /device:TPU:0, one launch (start us, length us, event | category | flops | bytes accessed | tf_op | source)
XLA Modules:
  0.0 820.1 jit_solution(6094621009104755735)
XLA Ops:
  6.5 13.1 %copy.80 = bf16[3,256,4096]{1,0,2:T(4,128)(2,1)} copy(bf16[3,256,4096]{2,1,0:T(8,128)(2,1)} %param.7) | data formatting | bytes 12582912 | tf_op args[0]
  19.6 7.1 all-to-all-start
  30.8 89.8 %all-to-all-done = bf16[3,256,4096]{1,0,2:T(4,128)(2,1)} async-done(((bf16[3,256,4096]{1,0,2:T(4,128)(2,1)}), bf16[3,256,4096]{1,0,2:T(4,128)(2,1)}, u32[]{:S(2)}, u32[]{:S(2)}) %all-to-all-start) | async-done | bytes 6291488 | tf_op jit(solution)/shard_map/all_to_all | solution.py:56
  120.6 7.0 copy.81
  127.5 8.7 %copy.82 = bf16[3,2,256,2048]{3,2,1,0:T(8,128)(2,1)} copy(bf16[3,2,256,2048]{2,3,1,0:T(8,128)(2,1)} %bitcast.174) | data formatting | bytes 12582912 | tf_op jit(solution)/shard_map/all_to_all | solution.py:56
  136.2 11.5 %copy.83 = bf16[3,512,2048]{2,0,1:T(4,128)(2,1)} copy(bf16[3,512,2048]{2,1,0:T(8,128)(2,1)} %bitcast.175) | data formatting | bytes 12582912 | tf_op jit(solution)/shard_map/all_to_all | solution.py:56
  147.7 24.3 %gather_fusion = bf16[640,3,2048]{2,1,0:T(4,128)(2,1)} fusion(bf16[3,512,2048]{2,0,1:T(4,128)(2,1)} %copy.83, s32[1024]{0:T(1024)S(1)} %pad_clamp_fusion.1), kind=kCustom, calls=%fused_computation | custom fusion | bytes 15731200 | tf_op jit(solution)/shard_map/jit(_take)/gather | solution.py:57
  172.0 7.5 broadcast_select_fusion
  179.5 6.5 constant_dynamic-slice_fusion
  196.5 2.6 collective-permute-start.5
  204.5 7.3 collective-permute-done.2
  211.8 2.7 collective-permute-start.7
  216.3 3.6 collective-permute-start.9
  220.7 26.5 %collective-permute-done.5 = bf16[3,1,40,2048]{3,2,0,1:T(8,128)(2,1)S(1)} collective-permute-done((bf16[3,1,40,2048]{3,2,0,1:T(8,128)(2,1)S(1)}, bf16[3,1,40,2048]{3,2,0,1:T(8,128)(2,1)S(1)}, u32[]{:S(2)}, u32[]{:S(2)}) %collective-permute-start.5) | collective-permute-done | bytes 491552 | tf_op jit(solution)/shard_map/ppermute | solution.py:65
  248.1 8.5 %collective-permute-done.6 = bf16[3,1,40,2048]{3,2,0,1:T(8,128)(2,1)S(1)} collective-permute-done((bf16[3,1,40,2048]{3,2,0,1:T(8,128)(2,1)S(1)}, bf16[3,1,40,2048]{3,2,0,1:T(8,128)(2,1)S(1)}, u32[]{:S(2)}, u32[]{:S(2)}) %collective-permute-start.6) | collective-permute-done | bytes 491552 | tf_op jit(solution)/shard_map/ppermute | solution.py:65
  258.8 2.2 collective-permute-start.12
  261.8 42.6 %collective-permute-start.13 = (bf16[3,1,40,2048]{3,2,0,1:T(8,128)(2,1)S(1)}, bf16[3,1,40,2048]{3,2,0,1:T(8,128)(2,1)S(1)}, u32[]{:S(2)}, u32[]{:S(2)}) collective-permute-start(bf16[3,1,40,2048]{3,2,0,1:T(8,128)(2,1)S(1)} %bitcast.212), channel_id=1, source_target_pairs={{0,28},{2,30},{4,24},{6,26},{8,20},{10,22},{12,16},{14,18},{16,12}... | collective-permute-start | bytes 1474568 | tf_op jit(solution)/shard_map/ppermute | solution.py:65
  305.3 17.3 %collective-permute-done.9 = bf16[3,1,40,2048]{3,2,0,1:T(8,128)(2,1)S(1)} collective-permute-done((bf16[3,1,40,2048]{3,2,0,1:T(8,128)(2,1)S(1)}, bf16[3,1,40,2048]{3,2,0,1:T(8,128)(2,1)S(1)}, u32[]{:S(2)}, u32[]{:S(2)}) %collective-permute-start.9) | collective-permute-done | bytes 491552 | tf_op jit(solution)/shard_map/ppermute | solution.py:65
  322.6 2.6 collective-permute-start.14
  326.0 16.9 %collective-permute-done.10 = bf16[3,1,40,2048]{3,2,0,1:T(8,128)(2,1)S(1)} collective-permute-done((bf16[3,1,40,2048]{3,2,0,1:T(8,128)(2,1)S(1)}, bf16[3,1,40,2048]{3,2,0,1:T(8,128)(2,1)S(1)}, u32[]{:S(2)}, u32[]{:S(2)}) %collective-permute-start.10) | collective-permute-done | bytes 491552 | tf_op jit(solution)/shard_map/ppermute | solution.py:65
  347.2 17.6 %gather_fusion.1 = bf16[16,3,40,2048]{3,2,1,0:T(8,128)(2,1)} fusion(bf16[16,3,40,2048]{3,2,1,0:T(8,128)(2,1)} %bitcast.39, s32[1024]{0:T(1024)S(1)} %pad_clamp_fusion), kind=kCustom, calls=%fused_computation.1 | custom fusion | bytes 15728704 | tf_op jit(solution)/shard_map/gather | solution.py:66
  364.7 4.2 copy.100
  368.9 25.3 %copy.101 = bf16[640,3,2048]{2,1,0:T(4,128)(2,1)} copy(bf16[640,3,2048]{2,0,1:T(8,128)(2,1)S(1)} %bitcast.173) | data formatting | bytes 15728640 | tf_op jit(solution)/shard_map/reshape;reshape | solution.py:41
  394.3 7.6 broadcast_in_dim.179
  401.9 85.1 %scatter_fusion = bf16[3,512,2048]{2,0,1:T(4,128)(2,1)} fusion(bf16[3,512,2048]{2,0,1:T(4,128)(2,1)} %broadcast_in_dim.179, s32[640]{0:T(1024)S(1)} %fusion.213, bf16[640,3,2048]{2,1,0:T(4,128)(2,1)} %copy.101), kind=kCustom, calls=%fused_computation.2 | custom fusion | bytes 23595520 | tf_op jit(solution)/shard_map/scatter | solution.py:44
  487.0 20.8 %fusion.233 = (bf16[1,512,2048]{2,0,1:T(2,128)(2,1)}, bf16[1,512,2048]{2,0,1:T(2,128)(2,1)}, bf16[1,512,2048]{2,0,1:T(2,128)(2,1)}) fusion(bf16[3,512,2048]{2,0,1:T(4,128)(2,1)} %scatter_fusion), kind=kLoop, calls=%fused_computation.352 | loop fusion | bytes 12582912 | tf_op jit(solution)/shard_map/slice | solution.py:69
  507.7 9.0 %copy.102 = bf16[1,512,2048]{1,2,0:T(8,128)(2,1)S(1)} copy(bf16[1,512,2048]{2,0,1:T(2,128)(2,1)} %get-tuple-element.146) | data formatting | bytes 4194304 | tf_op jit(solution)/shard_map/slice | solution.py:69
  516.7 10.5 %copy.103 = bf16[1,512,2048]{1,2,0:T(8,128)(2,1)} copy(bf16[1,512,2048]{2,0,1:T(2,128)(2,1)} %get-tuple-element.147) | data formatting | bytes 4194304 | tf_op jit(solution)/shard_map/slice | solution.py:69
  527.2 3.3 fusion.1
  532.7 64.2 %all-reduce = f32[16]{0:T(128)S(1)} all-reduce(f32[16]{0:T(128)S(1)} %dynamic-update-slice), channel_id=1, replica_groups=mesh['seq'=16,'head'=2] {'seq'}, use_global_device_ids=true, to_apply=%add | all-reduce | flops 16 | bytes 128
  596.9 3.6 copy.129
  600.5 6.9 copy_bitcast_fusion
  607.4 87.7 %all-gather.3.cloned.1.call-done = f32[256,128,128]{2,1,0:T(8,128)} async-done(((f32[16,128,128]{2,1,0:T(8,128)}), f32[256,128,128]{2,1,0:T(8,128)}) %all-gather.3.cloned.1.call-update) | async-done | bytes 16777232 | tf_op jit(solution)/shard_map/all_gather | solution.py:23
  695.1 56.6 %while.14 = (s32[]{:T(128)}, f32[16,128,128]{2,1,0:T(8,128)S(1)}, s32[]{:T(128)}, f32[16,16,128,128]{3,2,1,0:T(8,128)}, f32[16]{0:T(128)S(1)}, /*index=5*/s32[]{:T(128)}, f32[1]{0:T(128)}, s32[]{:T(128)}) while((s32[]{:T(128)}, f32[16,128,128]{2,1,0:T(8,128)S(1)}, s32[]{:T(128)}, f32[16,16,128,128]{3,2,1,0:T(8,128)}, ...), condition=%wide.region_6.7_spmd.clone, body=%wide.region_5.6_spmd.clone.sunk | while | flops 1048581 | bytes 3145873 | solution.py:35
  696.4 2.1 fusion.301
  699.9 2.1 fusion.301
  703.5 2.1 fusion.301
  707.0 2.1 fusion.301
  710.5 2.1 fusion.301
  714.0 2.1 fusion.301
  717.6 2.1 fusion.301
  721.1 2.1 fusion.301
  724.6 2.1 fusion.301
  728.1 2.1 fusion.301
  731.7 2.1 fusion.301
  735.2 2.1 fusion.301
  738.7 2.1 fusion.301
  745.8 2.1 fusion.301
  769.6 2.4 multiply_reduce_fusion.4
  772.0 2.3 multiply_reduce_fusion.5
  774.3 2.3 multiply_reduce_fusion.6
  776.6 2.3 multiply_reduce_fusion.7
  778.9 2.3 multiply_reduce_fusion.8
  781.1 2.3 multiply_reduce_fusion.9
  783.4 2.3 multiply_reduce_fusion.10
  785.7 2.3 multiply_reduce_fusion.11
  788.0 2.3 multiply_reduce_fusion.12
  790.3 2.3 multiply_reduce_fusion.13
  792.6 2.3 multiply_reduce_fusion.14
  794.9 2.3 multiply_reduce_fusion.15
  797.1 2.3 multiply_reduce_fusion
  799.4 2.2 multiply_reduce_fusion.2
  801.6 2.2 multiply_reduce_fusion.1
  810.5 2.4 copy.105
  (200 shorter events, 72.1 us)
Async XLA Ops:
  19.6 7.2 copy-start.28
  19.6 8.8 %copy-start.26 = (s32[1,16,40]{2,1,0:T(8,128)S(1)}, s32[1,16,40]{2,1,0:T(8,128)}, u32[]{:S(2)}) copy-start(s32[1,16,40]{2,1,0:T(8,128)} %param.9) | copy-start | bytes 7684
  19.6 8.8 %copy-start.25 = (s32[1,16,40]{2,1,0:T(8,128)S(1)}, s32[1,16,40]{2,1,0:T(8,128)}, u32[]{:S(2)}) copy-start(s32[1,16,40]{2,1,0:T(8,128)} %param.8) | copy-start | bytes 7684
  19.6 101.0 %all-to-all-start = ((bf16[3,256,4096]{1,0,2:T(4,128)(2,1)}), bf16[3,256,4096]{1,0,2:T(4,128)(2,1)}, u32[]{:S(2)}, u32[]{:S(2)}) async-start(bf16[3,256,4096]{1,0,2:T(4,128)(2,1)} %copy.80), calls=%async_computation | async-start | bytes 16777216 | tf_op jit(solution)/shard_map/all_to_all | solution.py:56
  26.7 668.4 %all-gather.3.cloned.1.call-start = ((), (), s32[]{:S(2)}) async-start(), calls=%async_computation.1 | async-start | bytes 17825792 | tf_op jit(solution)/shard_map/all_gather | solution.py:23
  186.4 10.0 %collective-permute-start = (bf16[3,1,40,2048]{3,2,0,1:T(8,128)(2,1)S(1)}, bf16[3,1,40,2048]{3,2,0,1:T(8,128)(2,1)S(1)}, u32[]{:S(2)}, u32[]{:S(2)}) collective-permute-start(bf16[3,1,40,2048]{3,2,0,1:T(8,128)(2,1)S(1)} %bitcast.224), channel_id=1, source_target_pairs={{0,2},{2,0},{4,6},{6,4},{8,10},{10,8},{12,14},{14,12},{16,18},{18,... | collective-permute-start | bytes 1474568 | tf_op jit(solution)/shard_map/ppermute | solution.py:65
  188.0 14.1 %collective-permute-start.1 = (bf16[3,1,40,2048]{3,2,0,1:T(8,128)(2,1)S(1)}, bf16[3,1,40,2048]{3,2,0,1:T(8,128)(2,1)S(1)}, u32[]{:S(2)}, u32[]{:S(2)}) collective-permute-start(bf16[3,1,40,2048]{3,2,0,1:T(8,128)(2,1)S(1)} %bitcast.225), channel_id=1, source_target_pairs={{0,4},{2,6},{4,0},{6,2},{8,12},{10,14},{12,8},{14,10},{16,20},{18,... | collective-permute-start | bytes 1474568 | tf_op jit(solution)/shard_map/ppermute | solution.py:65
  189.7 22.1 %collective-permute-start.2 = (bf16[3,1,40,2048]{3,2,0,1:T(8,128)(2,1)S(1)}, bf16[3,1,40,2048]{3,2,0,1:T(8,128)(2,1)S(1)}, u32[]{:S(2)}, u32[]{:S(2)}) collective-permute-start(bf16[3,1,40,2048]{3,2,0,1:T(8,128)(2,1)S(1)} %bitcast.222), channel_id=1, source_target_pairs={{0,6},{2,4},{4,2},{6,0},{8,14},{10,12},{12,10},{14,8},{16,22},{18,... | collective-permute-start | bytes 1474568 | tf_op jit(solution)/shard_map/ppermute | solution.py:65
  189.9 25.5 %collective-permute-start.3 = (bf16[3,1,40,2048]{3,2,0,1:T(8,128)(2,1)S(1)}, bf16[3,1,40,2048]{3,2,0,1:T(8,128)(2,1)S(1)}, u32[]{:S(2)}, u32[]{:S(2)}) collective-permute-start(bf16[3,1,40,2048]{3,2,0,1:T(8,128)(2,1)S(1)} %bitcast.220), channel_id=1, source_target_pairs={{0,8},{2,10},{4,12},{6,14},{8,0},{10,2},{12,4},{14,6},{16,24},{18,... | collective-permute-start | bytes 1474568 | tf_op jit(solution)/shard_map/ppermute | solution.py:65
  191.6 24.7 %collective-permute-start.4 = (bf16[3,1,40,2048]{3,2,0,1:T(8,128)(2,1)S(1)}, bf16[3,1,40,2048]{3,2,0,1:T(8,128)(2,1)S(1)}, u32[]{:S(2)}, u32[]{:S(2)}) collective-permute-start(bf16[3,1,40,2048]{3,2,0,1:T(8,128)(2,1)S(1)} %bitcast.218), channel_id=1, source_target_pairs={{0,10},{2,8},{4,14},{6,12},{8,2},{10,0},{12,6},{14,4},{16,26},{18,... | collective-permute-start | bytes 1474568 | tf_op jit(solution)/shard_map/ppermute | solution.py:65
  196.5 50.8 %collective-permute-start.5 = (bf16[3,1,40,2048]{3,2,0,1:T(8,128)(2,1)S(1)}, bf16[3,1,40,2048]{3,2,0,1:T(8,128)(2,1)S(1)}, u32[]{:S(2)}, u32[]{:S(2)}) collective-permute-start(bf16[3,1,40,2048]{3,2,0,1:T(8,128)(2,1)S(1)} %bitcast.223), channel_id=1, source_target_pairs={{0,12},{2,14},{4,8},{6,10},{8,4},{10,6},{12,0},{14,2},{16,28},{18,... | collective-permute-start | bytes 1474568 | tf_op jit(solution)/shard_map/ppermute | solution.py:65
  202.1 54.5 %collective-permute-start.6 = (bf16[3,1,40,2048]{3,2,0,1:T(8,128)(2,1)S(1)}, bf16[3,1,40,2048]{3,2,0,1:T(8,128)(2,1)S(1)}, u32[]{:S(2)}, u32[]{:S(2)}) collective-permute-start(bf16[3,1,40,2048]{3,2,0,1:T(8,128)(2,1)S(1)} %bitcast.221), channel_id=1, source_target_pairs={{0,14},{2,12},{4,10},{6,8},{8,6},{10,4},{12,2},{14,0},{16,30},{18,... | collective-permute-start | bytes 1474568 | tf_op jit(solution)/shard_map/ppermute | solution.py:65
  211.8 47.0 %collective-permute-start.7 = (bf16[3,1,40,2048]{3,2,0,1:T(8,128)(2,1)S(1)}, bf16[3,1,40,2048]{3,2,0,1:T(8,128)(2,1)S(1)}, u32[]{:S(2)}, u32[]{:S(2)}) collective-permute-start(bf16[3,1,40,2048]{3,2,0,1:T(8,128)(2,1)S(1)} %bitcast.219), channel_id=1, source_target_pairs={{0,16},{2,18},{4,20},{6,22},{8,24},{10,26},{12,28},{14,30},{16,0},... | collective-permute-start | bytes 1474568 | tf_op jit(solution)/shard_map/ppermute | solution.py:65
  215.4 46.4 %collective-permute-start.8 = (bf16[3,1,40,2048]{3,2,0,1:T(8,128)(2,1)S(1)}, bf16[3,1,40,2048]{3,2,0,1:T(8,128)(2,1)S(1)}, u32[]{:S(2)}, u32[]{:S(2)}) collective-permute-start(bf16[3,1,40,2048]{3,2,0,1:T(8,128)(2,1)S(1)} %bitcast.217), channel_id=1, source_target_pairs={{0,18},{2,16},{4,22},{6,20},{8,26},{10,24},{12,30},{14,28},{16,2},... | collective-permute-start | bytes 1474568 | tf_op jit(solution)/shard_map/ppermute | solution.py:65
  216.3 106.3 %collective-permute-start.9 = (bf16[3,1,40,2048]{3,2,0,1:T(8,128)(2,1)S(1)}, bf16[3,1,40,2048]{3,2,0,1:T(8,128)(2,1)S(1)}, u32[]{:S(2)}, u32[]{:S(2)}) collective-permute-start(bf16[3,1,40,2048]{3,2,0,1:T(8,128)(2,1)S(1)} %bitcast.216), channel_id=1, source_target_pairs={{0,20},{2,22},{4,16},{6,18},{8,28},{10,30},{12,24},{14,26},{16,4},... | collective-permute-start | bytes 1474568 | tf_op jit(solution)/shard_map/ppermute | solution.py:65
  247.3 95.7 %collective-permute-start.10 = (bf16[3,1,40,2048]{3,2,0,1:T(8,128)(2,1)S(1)}, bf16[3,1,40,2048]{3,2,0,1:T(8,128)(2,1)S(1)}, u32[]{:S(2)}, u32[]{:S(2)}) collective-permute-start(bf16[3,1,40,2048]{3,2,0,1:T(8,128)(2,1)S(1)} %bitcast.215), channel_id=1, source_target_pairs={{0,22},{2,20},{4,18},{6,16},{8,30},{10,28},{12,26},{14,24},{16,6},... | collective-permute-start | bytes 1474568 | tf_op jit(solution)/shard_map/ppermute | solution.py:65
  256.6 87.3 %collective-permute-start.11 = (bf16[3,1,40,2048]{3,2,0,1:T(8,128)(2,1)S(1)}, bf16[3,1,40,2048]{3,2,0,1:T(8,128)(2,1)S(1)}, u32[]{:S(2)}, u32[]{:S(2)}) collective-permute-start(bf16[3,1,40,2048]{3,2,0,1:T(8,128)(2,1)S(1)} %bitcast.214), channel_id=1, source_target_pairs={{0,24},{2,26},{4,28},{6,30},{8,16},{10,18},{12,20},{14,22},{16,8},... | collective-permute-start | bytes 1474568 | tf_op jit(solution)/shard_map/ppermute | solution.py:65
  258.8 85.9 %collective-permute-start.12 = (bf16[3,1,40,2048]{3,2,0,1:T(8,128)(2,1)S(1)}, bf16[3,1,40,2048]{3,2,0,1:T(8,128)(2,1)S(1)}, u32[]{:S(2)}, u32[]{:S(2)}) collective-permute-start(bf16[3,1,40,2048]{3,2,0,1:T(8,128)(2,1)S(1)} %bitcast.213), channel_id=1, source_target_pairs={{0,26},{2,24},{4,30},{6,28},{8,18},{10,16},{12,22},{14,20},{16,10}... | collective-permute-start | bytes 1474568 | tf_op jit(solution)/shard_map/ppermute | solution.py:65
  261.8 83.7 %collective-permute-start.13 = (bf16[3,1,40,2048]{3,2,0,1:T(8,128)(2,1)S(1)}, bf16[3,1,40,2048]{3,2,0,1:T(8,128)(2,1)S(1)}, u32[]{:S(2)}, u32[]{:S(2)}) collective-permute-start(bf16[3,1,40,2048]{3,2,0,1:T(8,128)(2,1)S(1)} %bitcast.212), channel_id=1, source_target_pairs={{0,28},{2,30},{4,24},{6,26},{8,20},{10,22},{12,16},{14,18},{16,12}... | collective-permute-start | bytes 1474568 | tf_op jit(solution)/shard_map/ppermute | solution.py:65
  322.6 23.7 %collective-permute-start.14 = (bf16[3,1,40,2048]{3,2,0,1:T(8,128)(2,1)S(1)}, bf16[3,1,40,2048]{3,2,0,1:T(8,128)(2,1)S(1)}, u32[]{:S(2)}, u32[]{:S(2)}) collective-permute-start(bf16[3,1,40,2048]{3,2,0,1:T(8,128)(2,1)S(1)} %bitcast.211), channel_id=1, source_target_pairs={{0,30},{2,28},{4,26},{6,24},{8,22},{10,20},{12,18},{14,16},{16,14}... | collective-permute-start | bytes 1474568 | tf_op jit(solution)/shard_map/ppermute | solution.py:65
  527.2 3.4 copy-start.29
  527.2 69.6 %copy-start.27 = (f32[2048]{0:T(1024)S(1)}, f32[2048]{0:T(1024)}, u32[]{:S(2)}) copy-start(f32[2048]{0:T(1024)} %param.11) | copy-start | bytes 24580
  596.9 3.6 copy-start
  767.9 4.1 copy-start.24
  769.6 4.7 copy-start.23
  772.0 4.6 copy-start.22
  774.3 4.6 copy-start.21
  776.6 4.6 copy-start.20
  778.8 4.6 copy-start.19
  781.1 4.6 copy-start.18
  783.4 4.6 copy-start.17
  785.7 4.6 copy-start.16
  788.0 4.6 copy-start.15
  790.3 4.6 copy-start.14
  792.5 4.6 copy-start.13
  794.8 4.6 copy-start.12
  797.1 4.5 copy-start.11
  803.9 5.5 copy-start.10
  803.9 5.6 copy-start.7
  803.9 5.7 copy-start.6
  803.9 5.8 copy-start.4
  803.9 5.9 copy-start.3
  803.9 6.0 copy-start.2
  805.1 5.0 copy-start.1
  807.2 3.0 copy-start.9
  808.3 2.0 copy-start.8
  809.4 1.0 copy-start.5
Sparse Core Ops, SparseCore 0:
  530.7 164.3 all-gather.2
